TPU v7x, 512 devices: a whole 4x8x8 slice. The times are simulated.
512 devices in a mesh: seq: 64 (over y, z), head: 8 (over x, core).
Axes of the slice: x: 4, y: 8, z: 8, core: 2. Of those that a mesh axis runs over, the one named last changes fastest.
Arguments:
- queries: bfloat16 [16384, 4096], P(('seq', 'head'))
- key_values: bfloat16 [16384, 2, 1024], P(('seq', 'head'))
- gate_logits: bfloat16 [16384, 4096], P(('seq', 'head')), may hold values from -6 to 6
- vertical_blocks: int32 [32, 16], replicated, may hold values from 0 to 255, as said below
- slash_offsets: int32 [32, 8], replicated, may hold values from 0 to 8, as said below
- slash_count: int32 [32], replicated, may hold values from 2 to 8, as said below
Outputs:
- gated: bfloat16 [16384, 4096], P(('seq', 'head'))
Inputs may be any that keep to these rules, and one draw needn't show every extreme that they name: `slash_count`: between 2 and 8; the largest and the smallest are reached. Heads are ranked by (slash_count[h], h) ascending, and rank r goes to head group (r % 8) if (r // 8) is even, else to group 8 - 1 - (r % 8). For each head, slash_offsets[h, 0] = 0 and the 8 offsets are distinct; the largest possible offset is used by some head. `vertical_blocks`: each head's 16 blocks lie in distinct token shards of 256 tokens (block b is in shard b // 4); the heads of one group, as defined with slash_count, have at most 1 vertical blocks in one shard together, and exactly 1 in some shard. The first and the last block of the stretch are used by some head.
All inputs are finite; a program needn't handle non-finite values.
Results may differ from a plain program's by a relative error of at most 0.0057.
Values may be sent and summed in bfloat16 or wider, within the bound.
No kernel may reach another device: no remote copies, remote signals or barrier semaphores. Data moves between devices by JAX's collectives and lax.ppermute only.
A program may use at most 64 MiB of HBM per device.

v0:
```python
import jax
import jax.numpy as jnp
from jax import lax
from jax.sharding import PartitionSpec as P

H = 32
KVH = 8
DH = 128
BLOCK = 64
NS = 8
REACH = 2


def from_behind(value, axis, steps):
    count = lax.axis_size(axis)
    first, last = (max(0, -steps), min(count, count - steps))
    return lax.ppermute(value, axis, [(source, source + steps) for source in range(first, last)])


def block_attend(
    q_rows,
    vert_keys,
    vert_vals,
    vert_ids,
    vert_live,
    slash_keys,
    slash_vals,
    offsets,
    slash_live,
    block_index,
):
    head_width = q_rows.shape[-1]
    score_scale = head_width ** (-0.5)
    positions = jnp.arange(q_rows.shape[0], dtype=jnp.int32)
    causal = positions[None, :] <= positions[:, None]
    vert_scores = (
        jnp.einsum("qd,skd->qsk", q_rows, vert_keys, preferred_element_type=jnp.float32)
        * score_scale
    )
    slash_scores = (
        jnp.einsum("qd,nkd->qnk", q_rows, slash_keys, preferred_element_type=jnp.float32)
        * score_scale
    )
    distance = block_index - vert_ids
    on_slash = jnp.any((distance[:, None] == offsets[None, :]) & slash_live[None, :], axis=1)
    vert_ok = vert_live & (vert_ids >= 0) & (vert_ids <= block_index) & jnp.logical_not(on_slash)
    vert_mask = vert_ok[None, :, None] & (
        (vert_ids < block_index)[None, :, None] | causal[:, None, :]
    )
    slash_ok = slash_live & (block_index - offsets >= 0)
    slash_mask = slash_ok[None, :, None] & ((offsets > 0)[None, :, None] | causal[:, None, :])
    vert_scores = jnp.where(vert_mask, vert_scores, -jnp.inf)
    slash_scores = jnp.where(slash_mask, slash_scores, -jnp.inf)
    row_max = jnp.maximum(jnp.max(vert_scores, axis=(1, 2)), jnp.max(slash_scores, axis=(1, 2)))
    vert_exp = jnp.exp(vert_scores - row_max[:, None, None])
    slash_exp = jnp.exp(slash_scores - row_max[:, None, None])
    row_total = jnp.sum(vert_exp, axis=(1, 2)) + jnp.sum(slash_exp, axis=(1, 2))
    vert_weight = (vert_exp / row_total[:, None, None]).astype(jnp.bfloat16)
    slash_weight = (slash_exp / row_total[:, None, None]).astype(jnp.bfloat16)
    result = jnp.einsum("qsk,skd->qd", vert_weight, vert_vals, preferred_element_type=jnp.float32)
    result = result + jnp.einsum(
        "qnk,nkd->qd", slash_weight, slash_vals, preferred_element_type=jnp.float32
    )
    return result.astype(jnp.bfloat16)


def group_order(counts, group_count):
    group_size = H // group_count
    ranking = jnp.argsort(counts * H + jnp.arange(H, dtype=jnp.int32), stable=True)
    index = jnp.arange(H, dtype=jnp.int32)
    group = index // group_size
    within = index % group_size
    rank_of = within * group_count + jnp.where(within % 2 == 0, group, group_count - 1 - group)
    return ranking[rank_of]


def body(queries, key_values, gate_logits, vertical_blocks, slash_offsets, slash_count):
    group_count = lax.axis_size("head")
    seq_rank = lax.axis_index("seq")
    group_rank = lax.axis_index("head")
    group_size = H // group_count
    tok_rows = queries.shape[0]
    tok_dev = tok_rows * group_count
    blocks_dev = tok_dev // BLOCK
    head_slot = group_order(slash_count, group_count)
    kv_index = head_slot // (H // KVH)
    my_heads = lax.dynamic_slice_in_dim(head_slot, group_rank * group_size, group_size)
    q_grouped = jnp.take(queries.reshape(tok_rows, H, DH), head_slot, axis=1)
    my_queries = lax.all_to_all(q_grouped, "head", split_axis=1, concat_axis=0, tiled=True)
    whole_pairs = lax.all_gather(key_values, "head", axis=0, tiled=True)
    my_kv = lax.dynamic_slice_in_dim(kv_index, group_rank * group_size, group_size)
    my_pairs = jnp.take(whole_pairs.reshape(tok_dev, 2, KVH, DH), my_kv, axis=2)
    earlier = []
    for distance in range(REACH, 0, -1):
        earlier.append(from_behind(my_pairs, "seq", distance))
    reach_keys = jnp.concatenate(earlier + [my_pairs], axis=0)
    reach_blocks = reach_keys.reshape((REACH + 1) * blocks_dev, BLOCK, 2, group_size, DH)
    pair_blocks = my_pairs.reshape(blocks_dev, BLOCK, 2, group_size, DH)
    my_vertical = jnp.take(vertical_blocks, my_heads, axis=0)
    owned = my_vertical // blocks_dev == seq_rank
    block_range = jnp.arange(blocks_dev, dtype=jnp.int32)
    owned_ids = jnp.max(jnp.where(owned, my_vertical, -1), axis=1)
    local_block = owned_ids - seq_rank * blocks_dev
    selector = ((local_block[:, None] == block_range[None, :]) & (owned_ids >= 0)[:, None]).astype(
        jnp.bfloat16
    )
    packed = jnp.einsum(
        "pt,tbxpd->pxbd", selector, pair_blocks, preferred_element_type=jnp.float32
    ).astype(jnp.bfloat16)
    vert_data, vert_all_ids = (
        lax.all_gather(packed[None], "seq", axis=0, tiled=True),
        lax.all_gather(owned_ids[None], "seq", axis=0, tiled=True),
    )

    def vertical_for(head_pos):
        chosen = lax.dynamic_index_in_dim(vert_data, head_pos, 1, keepdims=False)
        chosen_ids = lax.dynamic_index_in_dim(vert_all_ids, head_pos, 1, keepdims=False)
        return (chosen[:, 0], chosen[:, 1], chosen_ids, jnp.ones(chosen_ids.shape, dtype=bool))

    slot_range_ns = jnp.arange(NS, dtype=jnp.int32)
    my_offsets = jnp.take(slash_offsets, my_heads, axis=0)
    my_counts = jnp.take(slash_count, my_heads, axis=0)

    def head_pass(head_pos):
        vert_keys, vert_vals, vert_ids, vert_live = vertical_for(head_pos)
        head_queries = lax.dynamic_index_in_dim(my_queries, head_pos, 1, keepdims=False).reshape(
            blocks_dev, BLOCK, DH
        )
        head_reach = lax.dynamic_index_in_dim(reach_blocks, head_pos, 3, keepdims=False)
        offsets = lax.dynamic_index_in_dim(my_offsets, head_pos, 0, keepdims=False)
        slash_live = slot_range_ns < lax.dynamic_index_in_dim(
            my_counts, head_pos, 0, keepdims=False
        )

        def query_pass(inputs):
            q_rows, local_index = inputs
            block_index = seq_rank * blocks_dev + local_index
            slash_index = REACH * blocks_dev + local_index - offsets
            slash_blocks = jnp.take(head_reach, slash_index, axis=0)
            return block_attend(
                q_rows,
                vert_keys,
                vert_vals,
                vert_ids,
                vert_live,
                slash_blocks[:, :, 0],
                slash_blocks[:, :, 1],
                offsets,
                slash_live,
                block_index,
            )

        return lax.map(query_pass, (head_queries, block_range))

    attended = lax.map(head_pass, jnp.arange(group_size, dtype=jnp.int32)).reshape(
        group_size, tok_dev, DH
    )
    returned = lax.all_to_all(attended, "head", split_axis=1, concat_axis=0, tiled=True)
    head_range_all = jnp.arange(H, dtype=jnp.int32)
    inverse = jnp.sum(
        jnp.where(head_slot[None, :] == head_range_all[:, None], head_range_all[None, :], 0), axis=1
    )
    natural = jnp.take(returned, inverse, axis=0)
    gate = jax.nn.sigmoid(gate_logits.astype(jnp.float32)).reshape(tok_rows, H, DH)
    gated = gate * jnp.transpose(natural, (1, 0, 2)).astype(jnp.float32)
    return gated.astype(jnp.bfloat16).reshape(tok_rows, H * DH)


def solution(mesh):
    in_specs = (
        P(("seq", "head"), None),
        P(("seq", "head"), None, None),
        P(("seq", "head"), None),
        P(),
        P(),
        P(),
    )
    out_specs = P(("seq", "head"), None)
    return jax.shard_map(body, mesh=mesh, in_specs=in_specs, out_specs=out_specs, check_vma=False)
```

profile of v0, /device:TPU:1, one launch (start us, length us, event | category | flops | bytes accessed | tf_op | source)
XLA Modules:
  0.0 331.5 jit_solution(11809386844297845460)
XLA Ops:
  6.5 0.7 all-gather.5.cloned.1.call-update
  7.3 0.8 copy.62
  8.1 0.7 iota_add_fusion
  8.7 1.6 sort.17
  10.4 0.7 gather_fusion.1
  12.1 32.1 %all-gather.5.cloned.1.call-done = bf16[256,2,1024]{2,1,0:T(2,128)(2,1)} async-done(((bf16[32,2,1024]{2,1,0:T(2,128)(2,1)}), bf16[256,2,1024]{2,1,0:T(2,128)(2,1)}) %all-gather.5.cloned.1.call-update) | async-done | bytes 1048592 | tf_op jit(solution)/shard_map/all_gather | solution.py:90
  44.1 2.4 copy.60
  46.5 0.7 copy.61
  47.2 0.6 gather_fusion.4
  48.5 0.7 copy.97
  49.9 0.8 select_bitcast_fusion
  50.7 3.6 %all-to-all-start = ((bf16[32,32,128]{2,0,1:T(8,128)(2,1)}), bf16[32,32,128]{2,0,1:T(8,128)(2,1)S(1)}, u32[]{:S(2)}, u32[]{:S(2)}) async-start(bf16[32,32,128]{2,0,1:T(8,128)(2,1)} %select_bitcast_fusion), calls=%async_computation | async-start | bytes 524288 | tf_op jit(solution)/shard_map/all_to_all | solution.py:89
  54.3 0.6 gather_fusion.6
  55.1 4.2 %collective-permute-start = (bf16[256,2,4,128]{3,0,1,2:T(8,128)(2,1)S(1)}, bf16[256,2,4,128]{3,0,1,2:T(8,128)(2,1)S(1)}, u32[]{:S(2)}, u32[]{:S(2)}) collective-permute-start(bf16[256,2,4,128]{3,0,1,2:T(8,128)(2,1)S(1)} %bitcast_select_fusion), channel_id=1, source_target_pairs={{0,16},{8,24},{16,32},{24,40},{32,48},{40,56},{48,64},{56,72},{64,... | collective-permute-start | bytes 1572872 | tf_op jit(solution)/shard_map/ppermute | solution.py:17
  59.3 3.3 collective-permute-start.1
  62.8 1.3 dynamic-slice
  64.9 45.2 %all-reduce = s32[256]{0:T(256)S(1)} all-reduce(s32[256]{0:T(256)S(1)} %dynamic-update-slice), channel_id=3, replica_groups=mesh['seq'=64,'head'=8] {'seq'}, use_global_device_ids=true, to_apply=%add | all-reduce | flops 256 | bytes 2048
  111.0 1.3 pad_maximum_fusion
  112.4 60.5 %all-gather.7.cloned.1.call-done = bf16[256,2,64,128]{3,2,1,0:T(8,128)(2,1)} async-done(((bf16[4,2,64,128]{3,2,1,0:T(8,128)(2,1)}), bf16[256,2,64,128]{3,2,1,0:T(8,128)(2,1)}) %all-gather.7.cloned.1.call-update) | async-done | bytes 8388624 | tf_op jit(solution)/shard_map/all_gather | solution.py:111
  172.9 136.7 %while.37 = (s32[]{:T(128)}, bf16[4,4,64,128]{3,2,1,0:T(8,128)(2,1)}, s32[4]{0:T(128)S(1)}, bf16[256,4,128]{2,0,1:T(8,128)(2,1)S(1)}, s32[4,8]{1,0:T(4,128)S(1)}...) while((s32[]{:T(128)}, ...), condition=%wide.region_11.12_spmd.clone.clone, body=%wide.region_3.11_spmd.clone.clone.sunk | while | flops 154098576 | bytes 21907556 | solution.py:155
  175.1 1.8 copy_bitcast_fusion.6
  176.9 1.5 slice_bitcast_fusion.8
  178.4 1.0 copy_bitcast_fusion.7
  179.4 0.6 dynamic_slice.125
  180.7 25.7 %while.38 = (s32[]{:T(128)}, bf16[4,64,128]{2,1,0:T(8,128)(2,1)S(1)}, s32[64]{0:T(128)S(1)}, s32[4]{0:T(128)S(1)}, s32[]{:T(128)}, /*index=5*/s32[8]{0:T(128)S(1...) while((s32[]{:T(128)}, ...), condition=%wide.region_10.10_spmd, body=%wide.region_4.9_spmd.sunk | while | flops 154098560 | bytes 12468941 | solution.py:153
  182.1 1.9 fusion.56
  188.5 1.9 fusion.56
  194.9 1.9 fusion.56
  201.4 1.9 fusion.56
  206.4 0.6 bitcast_dynamic-update-slice_fusion.2
  209.3 1.8 copy_bitcast_fusion.6
  211.1 1.5 slice_bitcast_fusion.8
  212.5 1.0 copy_bitcast_fusion.7
  213.6 0.6 dynamic_slice.125
  214.9 25.7 %while.38 = (s32[]{:T(128)}, bf16[4,64,128]{2,1,0:T(8,128)(2,1)S(1)}, s32[64]{0:T(128)S(1)}, s32[4]{0:T(128)S(1)}, s32[]{:T(128)}, /*index=5*/s32[8]{0:T(128)S(1...) while((s32[]{:T(128)}, ...), condition=%wide.region_10.10_spmd, body=%wide.region_4.9_spmd.sunk | while | flops 154098560 | bytes 12468941 | solution.py:153
  216.2 1.9 fusion.56
  222.7 1.9 fusion.56
  229.1 1.9 fusion.56
  235.5 1.9 fusion.56
  240.6 0.6 bitcast_dynamic-update-slice_fusion.2
  243.5 1.8 copy_bitcast_fusion.6
  245.2 1.5 slice_bitcast_fusion.8
  246.7 1.0 copy_bitcast_fusion.7
  247.8 0.6 dynamic_slice.125
  249.0 25.7 %while.38 = (s32[]{:T(128)}, bf16[4,64,128]{2,1,0:T(8,128)(2,1)S(1)}, s32[64]{0:T(128)S(1)}, s32[4]{0:T(128)S(1)}, s32[]{:T(128)}, /*index=5*/s32[8]{0:T(128)S(1...) while((s32[]{:T(128)}, ...), condition=%wide.region_10.10_spmd, body=%wide.region_4.9_spmd.sunk | while | flops 154098560 | bytes 12468941 | solution.py:153
  250.4 1.9 fusion.56
  256.8 1.9 fusion.56
  263.3 1.9 fusion.56
  269.7 1.9 fusion.56
  274.8 0.6 bitcast_dynamic-update-slice_fusion.2
  277.6 1.8 copy_bitcast_fusion.6
  279.4 1.5 slice_bitcast_fusion.8
  280.9 1.0 copy_bitcast_fusion.7
  281.9 0.6 dynamic_slice.125
  283.2 25.7 %while.38 = (s32[]{:T(128)}, bf16[4,64,128]{2,1,0:T(8,128)(2,1)S(1)}, s32[64]{0:T(128)S(1)}, s32[4]{0:T(128)S(1)}, s32[]{:T(128)}, /*index=5*/s32[8]{0:T(128)S(1...) while((s32[]{:T(128)}, ...), condition=%wide.region_10.10_spmd, body=%wide.region_4.9_spmd.sunk | while | flops 154098560 | bytes 12468941 | solution.py:153
  284.6 1.9 fusion.56
  291.0 1.9 fusion.56
  297.5 1.9 fusion.56
  303.9 1.9 fusion.56
  309.0 0.6 bitcast_dynamic-update-slice_fusion.2
  309.6 1.9 copy.66
  311.5 5.2 %all-to-all-start.1 = ((bf16[4,256,128]{2,0,1:T(4,128)(2,1)}), bf16[4,256,128]{2,0,1:T(4,128)(2,1)S(1)}, u32[]{:S(2)}, u32[]{:S(2)}) async-start(bf16[4,256,128]{2,0,1:T(4,128)(2,1)} %bitcast.26), calls=%async_computation.1 | async-start | bytes 524288 | tf_op jit(solution)/shard_map/all_to_all | solution.py:158
  316.7 6.4 %all-to-all-done.1 = bf16[4,256,128]{2,0,1:T(4,128)(2,1)S(1)} async-done(((bf16[4,256,128]{2,0,1:T(4,128)(2,1)}), bf16[4,256,128]{2,0,1:T(4,128)(2,1)S(1)}, u32[]{:S(2)}, u32[]{:S(2)}) %all-to-all-start.1) | async-done | bytes 262176 | tf_op jit(solution)/shard_map/all_to_all | solution.py:158
  323.8 0.9 copy_bitcast_fusion.2
  (380 shorter events, 60.2 us)
Async XLA Ops:
  6.5 42.7 %copy-start = (bf16[32,4096]{1,0:T(8,128)(2,1)S(1)}, bf16[32,4096]{1,0:T(8,128)(2,1)}, u32[]{:S(2)}) copy-start(bf16[32,4096]{1,0:T(8,128)(2,1)} %param.10) | copy-start | bytes 786436
  6.5 37.6 %all-gather.5.cloned.1.call-start = ((), (), s32[]{:S(2)}) async-start(), calls=%async_computation.2 | async-start | bytes 1179648 | tf_op jit(solution)/shard_map/all_gather | solution.py:90
  7.3 165.6 %all-gather.7.cloned.1.call-start = ((), (), s32[]{:S(2)}) async-start(), calls=%async_computation.3 | async-start | bytes 8519680 | tf_op jit(solution)/shard_map/all_gather | solution.py:111
  48.0 6.3 %copy-start.1 = (s32[32]{0:T(128)S(1)}, s32[32]{0:T(128)}, u32[]{:S(2)}) copy-start(s32[32]{0:T(128)} %param.15) | copy-start | bytes 388
  48.5 61.8 %copy-start.4 = (s32[32,8]{0,1:T(8,128)S(1)}, s32[32,8]{0,1:T(8,128)}, u32[]{:S(2)}) copy-start(s32[32,8]{0,1:T(8,128)} %param.14) | copy-start | bytes 3076
  50.7 60.3 %all-to-all-start = ((bf16[32,32,128]{2,0,1:T(8,128)(2,1)}), bf16[32,32,128]{2,0,1:T(8,128)(2,1)S(1)}, u32[]{:S(2)}, u32[]{:S(2)}) async-start(bf16[32,32,128]{2,0,1:T(8,128)(2,1)} %select_bitcast_fusion), calls=%async_computation | async-start | bytes 524288 | tf_op jit(solution)/shard_map/all_to_all | solution.py:89
  55.1 55.9 %collective-permute-start = (bf16[256,2,4,128]{3,0,1,2:T(8,128)(2,1)S(1)}, bf16[256,2,4,128]{3,0,1,2:T(8,128)(2,1)S(1)}, u32[]{:S(2)}, u32[]{:S(2)}) collective-permute-start(bf16[256,2,4,128]{3,0,1,2:T(8,128)(2,1)S(1)} %bitcast_select_fusion), channel_id=1, source_target_pairs={{0,16},{8,24},{16,32},{24,40},{32,48},{40,56},{48,64},{56,72},{64,... | collective-permute-start | bytes 1572872 | tf_op jit(solution)/shard_map/ppermute | solution.py:17
  59.3 51.7 %collective-permute-start.1 = (bf16[256,2,4,128]{3,0,1,2:T(8,128)(2,1)S(1)}, bf16[256,2,4,128]{3,0,1,2:T(8,128)(2,1)S(1)}, u32[]{:S(2)}, u32[]{:S(2)}) collective-permute-start(bf16[256,2,4,128]{3,0,1,2:T(8,128)(2,1)S(1)} %bitcast_select_fusion), channel_id=1, source_target_pairs={{0,8},{8,16},{16,24},{24,32},{32,40},{40,48},{48,56},{56,64},{64,7... | collective-permute-start | bytes 1572872 | tf_op jit(solution)/shard_map/ppermute | solution.py:17
  185.4 1.2 copy-start.2
  191.8 1.2 copy-start.2
  198.2 1.2 copy-start.2
  204.7 1.2 copy-start.2
  219.5 1.2 copy-start.2
  226.0 1.2 copy-start.2
  232.4 1.2 copy-start.2
  238.8 1.2 copy-start.2
  253.7 1.2 copy-start.2
  260.1 1.2 copy-start.2
  266.6 1.2 copy-start.2
  273.0 1.2 copy-start.2
  287.9 1.2 copy-start.2
  294.3 1.2 copy-start.2
  300.8 1.2 copy-start.2
  307.2 1.2 copy-start.2
  309.6 14.2 %copy-start.3 = (bf16[32,4096]{1,0:T(8,128)(2,1)S(1)}, bf16[32,4096]{1,0:T(8,128)(2,1)}, u32[]{:S(2)}) copy-start(bf16[32,4096]{1,0:T(8,128)(2,1)} %param.12) | copy-start | bytes 786436
  311.5 11.6 %all-to-all-start.1 = ((bf16[4,256,128]{2,0,1:T(4,128)(2,1)}), bf16[4,256,128]{2,0,1:T(4,128)(2,1)S(1)}, u32[]{:S(2)}, u32[]{:S(2)}) async-start(bf16[4,256,128]{2,0,1:T(4,128)(2,1)} %bitcast.26), calls=%async_computation.1 | async-start | bytes 524288 | tf_op jit(solution)/shard_map/all_to_all | solution.py:158
Sparse Core Ops, SparseCore 0:
  9.5 34.5 all-gather.4
  49.3 123.5 all-gather.6
where the time goes:
time: 334 us; the launch traced here: 332 us
  waiting for transfers between devices  99.8 us (30%)
  local copies, waits for them, and re-layouts  57.9 us (17%)
  matrix products  47.2 us (14%)
  blocking collectives  45.2 us (14%)
  loops' own time  27.9 us (8%)
  other arithmetic  23.1 us (7%)
  starting transfers between devices  16.3 us (5%)
  between operations  14.3 us (4%)
    all_gather x1, waiting for transfers between devices, body(): lax.all_gather(packed[None], 'seq', axis=0, tiled=True)  60.5 us
    unnamed x1, blocking collectives  45.2 us
    all_gather x1, waiting for transfers between devices, body(): whole_pairs = lax.all_gather(key_values, 'head', axis=0, tiled=True)  32.1 us
    dot_general x16, matrix products, block_attend(): jnp.einsum('qd,skd->qsk', q_rows, vert_keys, preferred_element_type=jnp.f...  30.9 us
    another operation x4, loops' own time, head_pass(): return lax.map(query_pass, (head_queries, block_range))  21 us
    dynamic_slice x20, local copies, waits for them, and re-layouts, body(): lax.map(head_pass, jnp.arange(group_size, dtype=jnp.int32))  12.1 us
    reduce_sum x32, other arithmetic, block_attend(): row_total = jnp.sum(vert_exp, axis=(1, 2)) + jnp.sum(slash_exp, axis=(1, 2))  10.5 us
    gather x16, local copies, waits for them, and re-layouts, query_pass(): slash_blocks = jnp.take(head_reach, slash_index, axis=0)  9.56 us
  transfers between devices with their start and end apart: 6, of which 3 were waited for; matrix products, arithmetic and copies ran while one was open for 3% of the time, Pallas kernels for 0%

commit v1 on v0

--- a/solution.py
+++ b/solution.py
@@ -87,7 +87,9 @@
     my_heads = lax.dynamic_slice_in_dim(head_slot, group_rank * group_size, group_size)
     q_grouped = jnp.take(queries.reshape(tok_rows, H, DH), head_slot, axis=1)
     my_queries = lax.all_to_all(q_grouped, "head", split_axis=1, concat_axis=0, tiled=True)
-    whole_pairs = lax.all_gather(key_values, "head", axis=0, tiled=True)
+    upper = jnp.stack([key_values] * lax.axis_size("head"), 0)
+    extra = lax.all_to_all(upper, "head", split_axis=0, concat_axis=0)
+    whole_pairs = jnp.concatenate(extra, 0)
     my_kv = lax.dynamic_slice_in_dim(kv_index, group_rank * group_size, group_size)
     my_pairs = jnp.take(whole_pairs.reshape(tok_dev, 2, KVH, DH), my_kv, axis=2)
     earlier = []

time: 334 us -> 322 us (0.964)
  waiting for transfers between devices: 99.8 us -> 77.9 us
  starting transfers between devices: 16.3 us -> 25.1 us
    all_gather x1 -> x0, waiting for transfers between devices: 32.1 us -> none  [body(): whole_pairs = lax.all_gather(key_values, 'head', axis=0, tiled=True)]
    all_to_all x0 -> x1, waiting for transfers between devices: none -> 11.6 us  [body(): extra = lax.all_to_all(upper, 'head', split_axis=0, concat_axis=0)]
    all_to_all x0 -> x1, starting transfers between devices: none -> 10.3 us  [body(): extra = lax.all_to_all(upper, 'head', split_axis=0, concat_axis=0)]
where the time goes in v1:
time: 322 us; the launch traced here: 320 us
  waiting for transfers between devices  77.9 us (24%)
  local copies, waits for them, and re-layouts  56.7 us (18%)
  blocking collectives  48.1 us (15%)
  matrix products  47.1 us (15%)
  loops' own time  27.9 us (9%)
  starting transfers between devices  25.1 us (8%)
  other arithmetic  22.4 us (7%)
  between operations  14.3 us (4%)
    all_gather x1, waiting for transfers between devices, body(): lax.all_gather(packed[None], 'seq', axis=0, tiled=True)  59.9 us
    unnamed x1, blocking collectives  48.1 us
    dot_general x16, matrix products, block_attend(): jnp.einsum('qd,skd->qsk', q_rows, vert_keys, preferred_element_type=jnp.f...  30.9 us
    another operation x4, loops' own time, head_pass(): return lax.map(query_pass, (head_queries, block_range))  21 us
    dynamic_slice x20, local copies, waits for them, and re-layouts, body(): lax.map(head_pass, jnp.arange(group_size, dtype=jnp.int32))  12.1 us
    all_to_all x1, waiting for transfers between devices, body(): extra = lax.all_to_all(upper, 'head', split_axis=0, concat_axis=0)  11.6 us
    reduce_sum x32, other arithmetic, block_attend(): row_total = jnp.sum(vert_exp, axis=(1, 2)) + jnp.sum(slash_exp, axis=(1, 2))  10.5 us
    all_to_all x1, starting transfers between devices, body(): extra = lax.all_to_all(upper, 'head', split_axis=0, concat_axis=0)  10.3 us
  transfers between devices with their start and end apart: 6, of which 3 were waited for; matrix products, arithmetic and copies ran while one was open for 3% of the time, Pallas kernels for 0%

profile of v1, /device:TPU:1, one launch (start us, length us, event | category | flops | bytes accessed | tf_op | source)
XLA Modules:
  0.0 319.5 jit_solution(15277183083690456797)
XLA Ops:
  6.5 1.0 copy.61
  7.5 1.1 stack.2
  8.6 10.3 %all-to-all-start.1 = ((bf16[8,32,2,1024]{3,1,2,0:T(8,128)(2,1)}), bf16[8,32,2,1024]{3,1,2,0:T(8,128)(2,1)S(1)}, u32[]{:S(2)}, u32[]{:S(2)}) async-start(bf16[8,32,2,1024]{3,1,2,0:T(8,128)(2,1)} %stack.2), calls=%async_computation.1 | async-start | bytes 2097152 | tf_op jit(solution)/shard_map/all_to_all | solution.py:91
  19.0 1.6 sort.17
  20.6 0.7 gather_fusion.1
  22.4 11.6 %all-to-all-done.1 = bf16[8,32,2,1024]{3,1,2,0:T(8,128)(2,1)S(1)} async-done(((bf16[8,32,2,1024]{3,1,2,0:T(8,128)(2,1)}), bf16[8,32,2,1024]{3,1,2,0:T(8,128)(2,1)S(1)}, u32[]{:S(2)}, u32[]{:S(2)}) %all-to-all-start.1) | async-done | bytes 1048608 | tf_op jit(solution)/shard_map/all_to_all | solution.py:91
  34.5 0.6 gather_fusion.4
  35.8 0.7 copy.100
  37.2 0.8 select_bitcast_fusion
  38.0 4.3 %all-to-all-start = ((bf16[32,32,128]{2,0,1:T(8,128)(2,1)}), bf16[32,32,128]{2,0,1:T(8,128)(2,1)S(1)}, u32[]{:S(2)}, u32[]{:S(2)}) async-start(bf16[32,32,128]{2,0,1:T(8,128)(2,1)} %select_bitcast_fusion), calls=%async_computation | async-start | bytes 524288 | tf_op jit(solution)/shard_map/all_to_all | solution.py:89
  42.3 0.6 gather_fusion.6
  43.1 1.3 collective-permute-start
  44.4 4.0 %collective-permute-start.1 = (bf16[256,2,4,128]{3,0,1,2:T(8,128)(2,1)S(1)}, bf16[256,2,4,128]{3,0,1,2:T(8,128)(2,1)S(1)}, u32[]{:S(2)}, u32[]{:S(2)}) collective-permute-start(bf16[256,2,4,128]{3,0,1,2:T(8,128)(2,1)S(1)} %bitcast_select_fusion), channel_id=1, source_target_pairs={{0,8},{8,16},{16,24},{24,32},{32,40},{40,48},{48,56},{56,64},{64,7... | collective-permute-start | bytes 1572872 | tf_op jit(solution)/shard_map/ppermute | solution.py:17
  48.5 1.3 dynamic-slice
  50.7 48.1 %all-reduce = s32[256]{0:T(256)S(1)} all-reduce(s32[256]{0:T(256)S(1)} %dynamic-update-slice), channel_id=3, replica_groups=mesh['seq'=64,'head'=8] {'seq'}, use_global_device_ids=true, to_apply=%add | all-reduce | flops 256 | bytes 2048
  99.8 1.3 pad_maximum_fusion
  101.1 59.9 %all-gather.4.cloned.1.call-done = bf16[256,2,64,128]{3,2,1,0:T(8,128)(2,1)} async-done(((bf16[4,2,64,128]{3,2,1,0:T(8,128)(2,1)}), bf16[256,2,64,128]{3,2,1,0:T(8,128)(2,1)}) %all-gather.4.cloned.1.call-update) | async-done | bytes 8388624 | tf_op jit(solution)/shard_map/all_gather | solution.py:113
  161.0 136.6 %while.37 = (s32[]{:T(128)}, bf16[4,4,64,128]{3,2,1,0:T(8,128)(2,1)}, s32[4]{0:T(128)S(1)}, bf16[256,4,128]{2,0,1:T(8,128)(2,1)S(1)}, s32[4,8]{1,0:T(4,128)S(1)}...) while((s32[]{:T(128)}, ...), condition=%wide.region_11.12_spmd.clone.clone, body=%wide.region_3.11_spmd.clone.clone.sunk | while | flops 154098576 | bytes 21907556 | solution.py:157
  163.2 1.8 copy_bitcast_fusion.6
  165.0 1.5 slice_bitcast_fusion.8
  166.5 1.0 copy_bitcast_fusion.7
  167.5 0.6 dynamic_slice.125
  168.8 25.7 %while.38 = (s32[]{:T(128)}, bf16[4,64,128]{2,1,0:T(8,128)(2,1)S(1)}, s32[64]{0:T(128)S(1)}, s32[4]{0:T(128)S(1)}, s32[]{:T(128)}, /*index=5*/s32[8]{0:T(128)S(1...) while((s32[]{:T(128)}, ...), condition=%wide.region_10.10_spmd, body=%wide.region_4.9_spmd.sunk | while | flops 154098560 | bytes 12468941 | solution.py:155
  170.2 1.9 fusion.56
  176.6 1.9 fusion.56
  183.0 1.9 fusion.56
  189.4 1.9 fusion.56
  194.5 0.6 bitcast_dynamic-update-slice_fusion.2
  197.3 1.8 copy_bitcast_fusion.6
  199.1 1.5 slice_bitcast_fusion.8
  200.6 1.0 copy_bitcast_fusion.7
  201.7 0.6 dynamic_slice.125
  202.9 25.7 %while.38 = (s32[]{:T(128)}, bf16[4,64,128]{2,1,0:T(8,128)(2,1)S(1)}, s32[64]{0:T(128)S(1)}, s32[4]{0:T(128)S(1)}, s32[]{:T(128)}, /*index=5*/s32[8]{0:T(128)S(1...) while((s32[]{:T(128)}, ...), condition=%wide.region_10.10_spmd, body=%wide.region_4.9_spmd.sunk | while | flops 154098560 | bytes 12468941 | solution.py:155
  204.3 1.9 fusion.56
  209.4 0.6 dynamic_slice.128
  210.7 1.9 fusion.56
  217.2 1.9 fusion.56
  223.6 1.9 fusion.56
  228.6 0.6 bitcast_dynamic-update-slice_fusion.2
  231.5 1.8 copy_bitcast_fusion.6
  233.3 1.5 slice_bitcast_fusion.8
  234.7 1.0 copy_bitcast_fusion.7
  235.8 0.6 dynamic_slice.125
  237.1 25.7 %while.38 = (s32[]{:T(128)}, bf16[4,64,128]{2,1,0:T(8,128)(2,1)S(1)}, s32[64]{0:T(128)S(1)}, s32[4]{0:T(128)S(1)}, s32[]{:T(128)}, /*index=5*/s32[8]{0:T(128)S(1...) while((s32[]{:T(128)}, ...), condition=%wide.region_10.10_spmd, body=%wide.region_4.9_spmd.sunk | while | flops 154098560 | bytes 12468941 | solution.py:155
  238.4 1.9 fusion.56
  244.9 1.9 fusion.56
  251.3 1.9 fusion.56
  256.4 0.6 dynamic_slice.128
  257.7 1.9 fusion.56
  262.8 0.6 bitcast_dynamic-update-slice_fusion.2
  265.6 1.8 copy_bitcast_fusion.6
  267.4 1.5 slice_bitcast_fusion.8
  268.9 1.0 copy_bitcast_fusion.7
  269.9 0.6 dynamic_slice.125
  271.2 25.7 %while.38 = (s32[]{:T(128)}, bf16[4,64,128]{2,1,0:T(8,128)(2,1)S(1)}, s32[64]{0:T(128)S(1)}, s32[4]{0:T(128)S(1)}, s32[]{:T(128)}, /*index=5*/s32[8]{0:T(128)S(1...) while((s32[]{:T(128)}, ...), condition=%wide.region_10.10_spmd, body=%wide.region_4.9_spmd.sunk | while | flops 154098560 | bytes 12468941 | solution.py:155
  272.6 1.9 fusion.56
  279.0 1.9 fusion.56
  285.4 1.9 fusion.56
  291.9 1.9 fusion.56
  296.9 0.6 bitcast_dynamic-update-slice_fusion.2
  297.6 1.9 copy.68
  299.5 5.2 %all-to-all-start.2 = ((bf16[4,256,128]{2,0,1:T(4,128)(2,1)}), bf16[4,256,128]{2,0,1:T(4,128)(2,1)S(1)}, u32[]{:S(2)}, u32[]{:S(2)}) async-start(bf16[4,256,128]{2,0,1:T(4,128)(2,1)} %bitcast.25), calls=%async_computation.2 | async-start | bytes 524288 | tf_op jit(solution)/shard_map/all_to_all | solution.py:160
  304.7 6.4 %all-to-all-done.2 = bf16[4,256,128]{2,0,1:T(4,128)(2,1)S(1)} async-done(((bf16[4,256,128]{2,0,1:T(4,128)(2,1)}), bf16[4,256,128]{2,0,1:T(4,128)(2,1)S(1)}, u32[]{:S(2)}, u32[]{:S(2)}) %all-to-all-start.2) | async-done | bytes 262176 | tf_op jit(solution)/shard_map/all_to_all | solution.py:160
  311.8 0.9 copy_bitcast_fusion.2
  (384 shorter events, 59.4 us)
Async XLA Ops:
  6.5 30.0 %copy-start = (bf16[32,4096]{1,0:T(8,128)(2,1)S(1)}, bf16[32,4096]{1,0:T(8,128)(2,1)}, u32[]{:S(2)}) copy-start(bf16[32,4096]{1,0:T(8,128)(2,1)} %param.10) | copy-start | bytes 786436
  6.5 12.4 %copy-start.1 = (s32[32]{0:T(128)S(1)}, s32[32]{0:T(128)}, u32[]{:S(2)}) copy-start(s32[32]{0:T(128)} %param.15) | copy-start | bytes 388
  6.5 14.9 %copy-start.4 = (s32[32,16]{0,1:T(8,128)S(1)}, s32[32,16]{0,1:T(8,128)}, u32[]{:S(2)}) copy-start(s32[32,16]{0,1:T(8,128)} %param.13) | copy-start | bytes 6148
  8.6 25.3 %all-to-all-start.1 = ((bf16[8,32,2,1024]{3,1,2,0:T(8,128)(2,1)}), bf16[8,32,2,1024]{3,1,2,0:T(8,128)(2,1)S(1)}, u32[]{:S(2)}, u32[]{:S(2)}) async-start(bf16[8,32,2,1024]{3,1,2,0:T(8,128)(2,1)} %stack.2), calls=%async_computation.1 | async-start | bytes 2097152 | tf_op jit(solution)/shard_map/all_to_all | solution.py:91
  18.9 142.1 %all-gather.4.cloned.1.call-start = ((), (), s32[]{:S(2)}) async-start(), calls=%async_computation.3 | async-start | bytes 8519680 | tf_op jit(solution)/shard_map/all_gather | solution.py:113
  35.8 63.2 %copy-start.5 = (s32[32,8]{0,1:T(8,128)S(1)}, s32[32,8]{0,1:T(8,128)}, u32[]{:S(2)}) copy-start(s32[32,8]{0,1:T(8,128)} %param.14) | copy-start | bytes 3076
  38.0 61.7 %all-to-all-start = ((bf16[32,32,128]{2,0,1:T(8,128)(2,1)}), bf16[32,32,128]{2,0,1:T(8,128)(2,1)S(1)}, u32[]{:S(2)}, u32[]{:S(2)}) async-start(bf16[32,32,128]{2,0,1:T(8,128)(2,1)} %select_bitcast_fusion), calls=%async_computation | async-start | bytes 524288 | tf_op jit(solution)/shard_map/all_to_all | solution.py:89
  43.1 56.7 %collective-permute-start = (bf16[256,2,4,128]{3,0,1,2:T(8,128)(2,1)S(1)}, bf16[256,2,4,128]{3,0,1,2:T(8,128)(2,1)S(1)}, u32[]{:S(2)}, u32[]{:S(2)}) collective-permute-start(bf16[256,2,4,128]{3,0,1,2:T(8,128)(2,1)S(1)} %bitcast_select_fusion), channel_id=1, source_target_pairs={{0,16},{8,24},{16,32},{24,40},{32,48},{40,56},{48,64},{56,72},{64,... | collective-permute-start | bytes 1572872 | tf_op jit(solution)/shard_map/ppermute | solution.py:17
  44.4 55.4 %collective-permute-start.1 = (bf16[256,2,4,128]{3,0,1,2:T(8,128)(2,1)S(1)}, bf16[256,2,4,128]{3,0,1,2:T(8,128)(2,1)S(1)}, u32[]{:S(2)}, u32[]{:S(2)}) collective-permute-start(bf16[256,2,4,128]{3,0,1,2:T(8,128)(2,1)S(1)} %bitcast_select_fusion), channel_id=1, source_target_pairs={{0,8},{8,16},{16,24},{24,32},{32,40},{40,48},{48,56},{56,64},{64,7... | collective-permute-start | bytes 1572872 | tf_op jit(solution)/shard_map/ppermute | solution.py:17
  173.5 1.2 copy-start.2
  179.9 1.2 copy-start.2
  186.3 1.2 copy-start.2
  192.7 1.2 copy-start.2
  207.6 1.2 copy-start.2
  214.0 1.2 copy-start.2
  220.5 1.2 copy-start.2
  226.9 1.2 copy-start.2
  241.7 1.2 copy-start.2
  248.2 1.2 copy-start.2
  254.6 1.2 copy-start.2
  261.0 1.2 copy-start.2
  275.9 1.2 copy-start.2
  282.3 1.2 copy-start.2
  288.7 1.2 copy-start.2
  295.2 1.2 copy-start.2
  297.6 14.2 %copy-start.3 = (bf16[32,4096]{1,0:T(8,128)(2,1)S(1)}, bf16[32,4096]{1,0:T(8,128)(2,1)}, u32[]{:S(2)}) copy-start(bf16[32,4096]{1,0:T(8,128)(2,1)} %param.12) | copy-start | bytes 786436
  299.5 11.7 %all-to-all-start.2 = ((bf16[4,256,128]{2,0,1:T(4,128)(2,1)}), bf16[4,256,128]{2,0,1:T(4,128)(2,1)S(1)}, u32[]{:S(2)}, u32[]{:S(2)}) async-start(bf16[4,256,128]{2,0,1:T(4,128)(2,1)} %bitcast.25), calls=%async_computation.2 | async-start | bytes 524288 | tf_op jit(solution)/shard_map/all_to_all | solution.py:160
Sparse Core Ops, SparseCore 0:
  36.6 124.3 all-gather.3
